TPU v7x, 32 devices: a whole 2x2x4 slice. The times are simulated.
32 devices in a mesh: ctx: 8 (over y, x, core), fsdp: 4 (over z).
Axes of the slice: x: 2, y: 2, z: 4, core: 2. Of those that a mesh axis runs over, the one named last changes fastest.
Arguments:
- xbc: bfloat16 [4, 1024, 9216], P('fsdp', 'ctx'), may hold values from -6 to 6
- dt_raw: bfloat16 [4, 128, 1024], P('fsdp', None, 'ctx'), may hold values from -4 to 15
- dy: bfloat16 [4, 1024, 8192], P('fsdp', 'ctx'), may hold values from -6 to 6
- conv_params: float32 [5, 9216], replicated, may hold values from -3 to 3
- head_params: float32 [3, 128], replicated, may hold values from -13 to 1.5, as said below
Outputs:
- d_xbc: bfloat16 [4, 1024, 9216], P('fsdp', 'ctx')
- d_dt_raw: float32 [4, 128, 1024], P('fsdp', None, 'ctx')
- d_conv: float32 [5, 9216], replicated
- d_head: float32 [3, 128], replicated
Inputs may be any that keep to these rules, and one draw needn't show every extreme that they name: `head_params`: head parameters.
All inputs are finite; a program needn't handle non-finite values.
Results may differ from a plain program's by a relative error of at most 0.007.
Values may be sent and summed in bfloat16 or wider, within the bound.
A program may use at most 256 MiB of HBM per device.

v0:
```python
import jax
import jax.numpy as jnp
from jax import lax
from jax.sharding import PartitionSpec as P

HEADS = 128
HEAD_DIM = 64
STATE = 128
GROUPS = 4
CONV_W = 4
SPAN = 128
exact_prec = lax.Precision.HIGHEST


def shifted(block, axis, distance):
    devices = range(lax.axis_size(axis))
    route = [(i - distance, i) for i in devices if i - distance in devices]
    return lax.ppermute(block, axis, route)


def entering_2(value, axis, join, neutral, backward):
    count = lax.axis_size(axis)
    place = lax.axis_index(axis)
    ahead = count - 1 - place if backward else place
    gathered = jax.tree.map(
        lambda a, kind: lax.all_gather(a.astype(kind), axis), value, (jnp.bfloat16, jnp.bfloat16)
    )
    state = jax.tree.map(lambda a, e: jnp.zeros_like(a) + jnp.asarray(e, a.dtype), value, neutral)

    def one(hop, state):
        source = count - 1 - hop if backward else hop
        return join(
            state,
            jax.tree.map(
                lambda a, own: lax.dynamic_index_in_dim(a, source, 0, False).astype(own.dtype),
                gathered,
                value,
            ),
        )

    return lax.fori_loop(0, ahead, one, state)


def split_channels(activated):
    row_count = activated.shape[0]
    x_width = HEADS * HEAD_DIM
    bc_width = GROUPS * STATE
    x_heads = activated[:, :x_width].reshape(row_count, HEADS, HEAD_DIM)
    b_groups = activated[:, x_width : x_width + bc_width].reshape(row_count, GROUPS, STATE)
    c_groups = activated[:, x_width + bc_width :].reshape(row_count, GROUPS, STATE)
    return (x_heads, b_groups, c_groups)


def prepare(extended, dt_values, conv_params, head_params):
    row_count = extended.shape[0] - (CONV_W - 1)
    mixed_in = jnp.broadcast_to(conv_params[CONV_W][None, :], (row_count, extended.shape[1]))
    for offset in range(CONV_W):
        mixed_in = mixed_in + conv_params[offset][None, :] * extended[offset : offset + row_count]
    activated = jax.nn.silu(mixed_in)
    x_heads, b_groups, c_groups = split_channels(activated)
    step_size = jax.nn.softplus(dt_values + head_params[0][:, None])
    rates = step_size * jnp.exp(head_params[1])[:, None]
    return (x_heads, b_groups, c_groups, step_size, rates)


def span_outputs(x_heads, b_groups, c_groups, step_size, rates, head_params):
    row_count = x_heads.shape[0]
    block_count = row_count // SPAN
    per_group = HEADS // GROUPS
    x_blocks = x_heads.reshape(block_count, SPAN, HEADS, HEAD_DIM)
    b_blocks = b_groups.reshape(block_count, SPAN, GROUPS, STATE)
    c_blocks = c_groups.reshape(block_count, SPAN, GROUPS, STATE)
    d_blocks = step_size.reshape(HEADS, block_count, SPAN).transpose(1, 0, 2)
    l_blocks = rates.reshape(HEADS, block_count, SPAN).transpose(1, 0, 2)
    causal_mask = jnp.arange(SPAN)[:, None] >= jnp.arange(SPAN)[None, :]

    def advance(state_now, block):
        x_block, b_block, c_block, d_block, l_block = block
        running = jnp.cumsum(l_block, axis=1)
        spacing = jnp.where(causal_mask[None], running[:, :, None] - running[:, None, :], 0.0)
        fading = jnp.where(causal_mask[None], jnp.exp(-spacing), 0.0)
        scores = jnp.einsum("tgn,sgn->gts", c_block, b_block, precision=exact_prec)
        weights = (
            scores[:, None]
            * fading.reshape(GROUPS, per_group, SPAN, SPAN)
            * d_block.reshape(GROUPS, per_group, 1, SPAN)
        )
        x_grouped = x_block.reshape(SPAN, GROUPS, per_group, HEAD_DIM)
        outputs = jnp.einsum("gkts,sgkp->tgkp", weights, x_grouped, precision=exact_prec)
        carried = jnp.einsum(
            "tgn,gkpn->tgkp",
            c_block,
            state_now.reshape(GROUPS, per_group, HEAD_DIM, STATE),
            precision=exact_prec,
        )
        decay_rows = jnp.exp(-running).T.reshape(SPAN, GROUPS, per_group)[..., None]
        outputs = (outputs + carried * decay_rows).reshape(SPAN, HEADS, HEAD_DIM)
        tail_weight = (jnp.exp(running - running[:, -1:]) * d_block).T
        weighted = (tail_weight[:, :, None] * x_block).reshape(SPAN, GROUPS, per_group, HEAD_DIM)
        fresh_state = jnp.einsum("sgkp,sgn->gkpn", weighted, b_block, precision=exact_prec).reshape(
            HEADS, HEAD_DIM, STATE
        )
        state_next = jnp.exp(-running[:, -1])[:, None, None] * state_now + fresh_state
        return (state_next, outputs)

    initial = jnp.zeros((HEADS, HEAD_DIM, STATE), jnp.float32)
    _, outputs = lax.scan(advance, initial, (x_blocks, b_blocks, c_blocks, d_blocks, l_blocks))
    outputs = outputs.reshape(row_count, HEADS, HEAD_DIM) + head_params[2][None, :, None] * x_heads
    return outputs.reshape(row_count, HEADS * HEAD_DIM)


def end_state(x_heads, b_groups, step_size, rates):
    row_count = x_heads.shape[0]
    per_group = HEADS // GROUPS
    running = jnp.cumsum(rates, axis=1)
    tail_weight = (jnp.exp(running - running[:, -1:]) * step_size).T
    weighted = (tail_weight[:, :, None] * x_heads).reshape(row_count, GROUPS, per_group, HEAD_DIM)
    summed = jnp.einsum("sgkp,sgn->gkpn", weighted, b_groups, precision=exact_prec)
    return summed.reshape(HEADS, HEAD_DIM, STATE)


def entry_terms(c_groups, rates, entering):
    row_count = c_groups.shape[0]
    per_group = HEADS // GROUPS
    running = jnp.cumsum(rates, axis=1)
    carried = jnp.einsum(
        "tgn,gkpn->tgkp",
        c_groups,
        entering.reshape(GROUPS, per_group, HEAD_DIM, STATE),
        precision=exact_prec,
    )
    carried = carried * jnp.exp(-running).T.reshape(row_count, GROUPS, per_group)[..., None]
    passed = jnp.exp(-running[:, -1])[:, None, None] * entering
    return (carried.reshape(row_count, HEADS * HEAD_DIM), passed)


def state_pull(c_groups, rates, upstream_heads):
    row_count = c_groups.shape[0]
    per_group = HEADS // GROUPS
    running = jnp.cumsum(rates, axis=1)
    weighted = (jnp.exp(-running).T[:, :, None] * upstream_heads).reshape(
        row_count, GROUPS, per_group, HEAD_DIM
    )
    summed = jnp.einsum("tgkp,tgn->gkpn", weighted, c_groups, precision=exact_prec)
    return summed.reshape(HEADS, HEAD_DIM, STATE)


def combine_carry(earlier_pair, later_pair):
    return (
        earlier_pair[0] * later_pair[0],
        later_pair[0][:, None, None] * earlier_pair[1] + later_pair[1],
    )


def shards(xbc, dt_raw, dy, conv_params, head_params):
    rim_rows = CONV_W - 1
    row_count = xbc.shape[1]
    before = shifted(xbc[:, row_count - rim_rows :, :], "ctx", 1)
    extended = jnp.concatenate([before[0], xbc[0]], axis=0).astype(jnp.float32)
    pieces, prep_back = jax.vjp(
        prepare, extended, dt_raw[0].astype(jnp.float32), conv_params, head_params
    )
    x_heads, b_groups, c_groups, step_size, rates = pieces
    _, inner_back = jax.vjp(
        span_outputs, x_heads, b_groups, c_groups, step_size, rates, head_params
    )
    leaving_state, state_back = jax.vjp(end_state, x_heads, b_groups, step_size, rates)
    upstream = dy[0].astype(jnp.float32)
    pull_term = state_pull(c_groups, rates, upstream.reshape(row_count, HEADS, HEAD_DIM))
    fading = jnp.exp(-jnp.sum(rates, axis=1))
    identity_pair = (jnp.ones_like(fading), jnp.zeros_like(leaving_state))
    _, entering = entering_2((fading, leaving_state), "ctx", combine_carry, identity_pair, False)
    _, later_grad = entering_2((fading, pull_term), "ctx", combine_carry, identity_pair, True)
    _, entry_back = jax.vjp(entry_terms, c_groups, rates, entering)
    grad_x_inner, grad_b_inner, grad_c_inner, grad_step_inner, grad_rate_inner, grad_head_inner = (
        inner_back(upstream)
    )
    grad_x_state, grad_b_state, grad_step_state, grad_rate_state = state_back(later_grad)
    grad_c_entry, grad_rate_entry, _ = entry_back((upstream, later_grad))
    grad_ext, grad_dt, grad_conv, grad_head = prep_back(
        (
            grad_x_inner + grad_x_state,
            grad_b_inner + grad_b_state,
            grad_c_inner + grad_c_entry,
            grad_step_inner + grad_step_state,
            grad_rate_inner + grad_rate_state + grad_rate_entry,
        )
    )
    grad_head = grad_head + grad_head_inner
    returned_rim = shifted(grad_ext[None, :rim_rows].astype(jnp.bfloat16), "ctx", -1).astype(
        jnp.float32
    )
    own_rows = grad_ext[rim_rows:]
    own_rows = jnp.concatenate(
        [own_rows[: row_count - rim_rows], own_rows[row_count - rim_rows :] + returned_rim[0]],
        axis=0,
    )
    total_conv, total_head = lax.psum((grad_conv, grad_head), ("ctx", "fsdp"))
    return (own_rows[None].astype(jnp.bfloat16), grad_dt[None], total_conv, total_head)


def solution(mesh):
    return jax.shard_map(
        shards,
        mesh=mesh,
        in_specs=(P("fsdp", "ctx", None), P("fsdp", None, "ctx"), P("fsdp", "ctx", None), P(), P()),
        out_specs=(P("fsdp", "ctx", None), P("fsdp", None, "ctx"), P(), P()),
        check_vma=False,
    )
```

profile of v0, /device:TPU:8, one launch (start us, length us, event | category | flops | bytes accessed | tf_op | source)
XLA Modules:
  0.0 550.6 jit_solution(5632665170448419959)
XLA Ops:
  7.2 1.0 slice.83
  8.2 1.7 collective-permute-start
  9.9 1.8 fusion.119
  12.5 0.9 copy.66
  13.7 4.3 copy.69
  17.9 3.2 copy.65
  21.3 2.0 copy.68
  23.3 3.4 maximum_convert_fusion
  26.7 12.4 %fusion.11 = (f32[128,9216]{0,1:T(8,128)S(1)}, f32[128,9216]{0,1:T(8,128)}) fusion(f32[131,9216]{0,1:T(8,128)S(1)} %maximum_convert_fusion, f32[9216]{0:T(1024)S(1)} %bitcast.354, f32[9216]{0:T(1024)S(1)} %bitcast.356, f32[9216]{0:T(1024)S(1)} %bitcast.358, f32[9216]{0:T(1024)S(1)} %bitcast.352, f32[9216]{0:T(1024)S(1)} %bitcast.365), kind=kLoop, calls=%fused_computation.34 | loop fusion | flops 14155776 | bytes 28495872 | tf_op jit(solution)/shard_map/jvp(jit(silu))/mul | solution.py:59
  39.1 2.1 copy-done.5
  41.3 5.0 fusion.53
  46.4 8.9 %all-gather.1 = bf16[8,1,128]{2,1,0:T(2,128)(2,1)S(1)} all-gather(bf16[1,1,128]{2,1,0:T(2,128)(2,1)S(1)} %convert_bitcast_fusion.1), channel_id=2, replica_groups=mesh['ctx'=8,'fsdp'=4] {'ctx'}, dimensions={0}, use_global_device_ids=true | all-gather | bytes 2304 | tf_op jit(solution)/shard_map/all_gather | solution.py:26
  57.2 8.2 %fusion.1 = f32[4,32,128,64]{2,3,1,0:T(8,128)} fusion(bf16[4,32,64,128]{3,2,1,0:T(8,128)(2,1)S(1)} %bitcast.325, f32[4,128,128]{2,1,0:T(8,128)S(1)} %fusion.120, f32[4,32,128]{2,1,0:T(8,128)S(1)} %bitcast.371, f32[4,32,128]{2,1,0:T(8,128)S(1)} %bitcast.373, pred[128,128]{1,0:T(8,128)(4,1)S(1)} %iota_compare_fusion), kind=kOutput, calls=%fused_computation.9 | convolution fusion | flops 1623195648 | bytes 6701056 | tf_op jit(solution)/shard_map/transpose(jvp())/while/body/eval_jaxpr/gkts,sgkp->tgkp/dot_general | solution.py:89
  65.4 72.6 %all-gather.7.cloned.1.call-done = bf16[8,128,64,128]{3,2,1,0:T(8,128)(2,1)} async-done(((bf16[1,128,64,128]{3,2,1,0:T(8,128)(2,1)}), bf16[8,128,64,128]{3,2,1,0:T(8,128)(2,1)}) %all-gather.7.cloned.1.call-update) | async-done | bytes 16777232 | tf_op jit(solution)/shard_map/all_gather | solution.py:26
  138.0 2.6 broadcast.354.clone
  140.6 38.3 %while.21 = (s32[]{:T(128)}, f32[128,64,128]{2,1,0:T(8,128)}, s32[]{:T(128)}, bf16[8,128]{1,0:T(8,128)(2,1)S(1)}, bf16[8,128,64,128]{3,2,1,0:T(8,128)(2,1)}, /*index=5*/s32[]{:T(128)}, s32[]{:T(128)}, s32[]{:T(128)}, s32[]{:T(128)}) while((s32[]{:T(128)}, f32[128,64,128]{2,1,0:T(8,128)}, s32[]{:T(128)}, bf16[8,128]{1,0:T(8,128)(2,1)S(1)}, ...), condition=%wide.region_7.8_spmd, body=%wide.region_6.7_spmd.sunk | while | flops 3145862 | bytes 10487195 | solution.py:41
  140.6 5.4 convert_add_fusion.6
  146.0 5.4 convert_add_fusion.6
  151.5 5.4 convert_add_fusion.6
  156.9 5.4 convert_add_fusion.6
  162.4 5.4 convert_add_fusion.6
  167.8 5.4 convert_add_fusion.6
  173.2 5.4 convert_add_fusion.6
  178.9 5.5 fusion.121
  184.4 8.7 %fusion.23 = (f32[128,4,32]{0,2,1:T(8,128)S(1)}, f32[128,4,32]{0,2,1:T(8,128)S(1)}, f32[4,32,64,128]{3,2,1,0:T(8,128)}) fusion(f32[128,9216]{0,1:T(8,128)} %copy-done.5, f32[4,32,64,128]{3,2,1,0:T(8,128)S(1)} %fusion.121, f32[128,4,128,1]{0,2,3,1:T(8,128)S(1)} %bitcast.336), kind=kOutput, calls=%fused_computation.50 | convolution fusion | flops 1614774272 | bytes 12976128 | tf_op jit(solution)/shard_map/transpose(jvp())/while/body/eval_jaxpr/sgkp,sgn->gkpn/dot_general | solution.py:100
  194.2 9.4 %fusion.16 = (f32[8192]{0:T(1024)}, f32[128,8192]{0,1:T(8,128)S(1)}, f32[128,8192]{0,1:T(8,128)}) fusion(bf16[1,128,8192]{1,2,0:T(8,128)(2,1)S(1)} %copy.65, f32[128,9216]{0,1:T(8,128)} %copy-done.5, f32[4,32,64,128]{3,2,1,0:T(8,128)} %copy-done.6, f32[128,128]{0,1:T(8,128)S(1)} %copy.73, f32[4,32,128,64]{2,3,1,0:T(8,128)} %fusion.1, ...), kind=kLoop, calls=%fused_computation.39 | loop fusion | flops 9428992 | bytes 27459584 | tf_op jit(solution)/shard_map/transpose(jvp())/reduce_sum | solution.py:108
  203.5 1.9 copy-done.4
  205.4 4.9 fusion.50
  210.8 3.8 fusion.21
  215.3 13.4 %fusion.37 = (f32[4,32,128]{2,1,0:T(8,128)}, f32[4,32,128]{2,1,0:T(8,128)}, f32[4,32,128]{2,1,0:T(8,128)}, f32[4,128,128]{2,1,0:T(8,128)S(1)}) fusion(f32[4,32,128]{2,1,0:T(8,128)S(1)} %bitcast.372, f32[4,32,128]{2,1,0:T(8,128)} %bitcast.374, f32[4,128,128]{2,1,0:T(8,128)} %copy-done.13, pred[128,128]{1,0:T(8,128)(4,1)} %copy-done.20, ...), kind=kOutput, calls=%fused_computation.65 | convolution fusion | flops 1646149632 | bytes 7159808 | tf_op jit(solution)/shard_map/transpose(jvp())/while/body/eval_jaxpr/gkts,sgkp->tgkp/dot_general | solution.py:89
  228.7 1.6 copy.92
  230.3 0.8 neg.196
  231.9 1.6 copy.87
  234.3 1.2 negate_bitcast_fusion
  235.4 1.6 fusion.94
  237.1 2.6 reduce_window_sum.53
  239.6 1.2 pad_add_fusion.2
  240.9 2.6 reduce_window_sum.54
  244.1 5.9 %fusion.68 = f32[128,4,128]{0,2,1:T(8,128)S(1)} fusion(f32[128,4,32,64]{0,3,2,1:T(8,128)} %bitcast.322, f32[128,4,32]{0,2,1:T(8,128)S(1)} %bitcast.351), kind=kOutput, calls=%fused_computation.95 | convolution fusion | flops 1611661312 | bytes 4521984 | tf_op jit(solution)/shard_map/transpose(jvp())/while/body/eval_jaxpr/sgkp,sgn->gkpn/dot_general | solution.py:100
  250.0 9.7 %fusion.54 = f32[128,4,128]{0,2,1:T(8,128)S(1)} fusion(f32[4,32,64,128]{3,2,1,0:T(8,128)S(1)} %bitcast.317, f32[128,4,32,64]{0,3,2,1:T(8,128)} %bitcast.323, f32[128,4,32]{0,2,1:T(8,128)S(1)} %bitcast.346), kind=kOutput, calls=%fused_computation.87 | convolution fusion | flops 1611661312 | bytes 8716288 | tf_op jit(solution)/shard_map/transpose(jvp(sgkp,sgn->gkpn))/dot_general | solution.py:118
  260.1 39.4 %all-gather.5.cloned.1.call-done = bf16[8,128,64,128]{3,2,1,0:T(8,128)(2,1)} async-done(((bf16[1,128,64,128]{3,2,1,0:T(8,128)(2,1)}), bf16[8,128,64,128]{3,2,1,0:T(8,128)(2,1)}) %all-gather.5.cloned.1.call-update) | async-done | bytes 16777232 | tf_op jit(solution)/shard_map/all_gather | solution.py:26
  299.5 2.5 broadcast.354
  301.9 9.9 %fusion.57 = f32[4,128,128]{1,2,0:T(8,128)} fusion(f32[4,32,64,128]{3,2,1,0:T(8,128)} %bitcast.318, bf16[128,4,32,64]{0,3,2,1:T(8,128)(2,1)S(1)} %bitcast.328, f32[128,4,32]{0,2,1:T(8,128)S(1)} %bitcast.350), kind=kOutput, calls=%fused_computation.88 | convolution fusion | flops 1612709888 | bytes 6619136 | tf_op jit(solution)/shard_map/transpose(jvp(tgn,gkpn->tgkp))/dot_general | solution.py:126
  311.9 4.2 fusion.20
  316.1 1.5 multiply_reduce_fusion.5
  318.4 1.1 reduce_window_sum.55
  319.6 1.9 fusion.112
  321.5 0.9 copy.67
  322.4 4.6 fusion.63
  327.0 1.6 fusion.62
  328.6 21.0 %multiply_reduce_fusion.4 = (f32[9216]{0:T(1024)S(1)}, f32[9216]{0:T(1024)S(1)}, f32[9216]{0:T(1024)S(1)}, f32[9216]{0:T(1024)S(1)}, f32[9216]{0:T(1024)S(1)}, /*index=5*/f32[128,9216]{0,1:T(8,128)S(1)}) fusion(f32[131,9216]{0,1:T(8,128)} %copy-done.3, f32[128,9216]{0,1:T(8,128)} %get-tuple-element.537, f32[128,8192]{0,1:T(8,128)} %get-tuple-element.546, ...), kind=kLoop, calls=%fused_computation.32 | loop fusion | flops 23546880 | bytes 33214464 | tf_op jit(solution)/shard_map/transpose(jvp())/reduce_sum | solution.py:58
  349.7 6.1 %broadcast_multiply_fusion.3 = (f32[128,9216]{0,1:T(8,128)S(1)}, f32[128,9216]{0,1:T(8,128)S(1)}, f32[128,9216]{0,1:T(8,128)S(1)}, f32[128,9216]{0,1:T(8,128)S(1)}) fusion(f32[128,9216]{0,1:T(8,128)S(1)} %get-tuple-element.531, f32[9216]{0:T(1024)S(1)} %bitcast.355, f32[9216]{0:T(1024)S(1)} %bitcast.353, f32[9216]{0:T(1024)S(1)} %bitcast.359, ...), kind=kLoop, calls=%fused_computation.73 | loop fusion | flops 4718592 | bytes 23740416 | tf_op jit(solution)/shard_map/transpose(jvp())/mul | solution.py:58
  355.8 9.4 %fusion.117 = (bf16[131,9216]{0,1:T(8,128)(2,1)S(1)}, f32[131,9216]{0,1:T(8,128)}) fusion(f32[128,9216]{0,1:T(8,128)S(1)} %get-tuple-element.541, f32[128,9216]{0,1:T(8,128)S(1)} %get-tuple-element.542, f32[128,9216]{0,1:T(8,128)S(1)} %get-tuple-element.543, f32[128,9216]{0,1:T(8,128)S(1)} %get-tuple-element.540), kind=kLoop, calls=%fused_computation.175 | loop fusion | flops 4829184 | bytes 26118144 | tf_op jit(solution)/shard_map/convert.12
  365.2 1.5 slice_bitcast_fusion
  367.5 2.1 copy.84
  369.6 1.3 collective-permute-start.1
  371.6 0.9 pad_add_fusion.1
  373.3 79.4 %psum.15 = f32[3,128]{1,0:T(4,128)} all-reduce(f32[3,128]{1,0:T(4,128)S(1)} %pad_add_fusion.3), channel_id=1, replica_groups=mesh['ctx'=8,'fsdp'=4] {'ctx','fsdp'}, use_global_device_ids=true, to_apply=%region_31.32 | all-reduce | flops 384 | bytes 3072 | tf_op jit(solution)/shard_map/psum | solution.py:198
  452.6 2.0 copy.85
  454.6 3.3 fusion.38
  457.9 2.4 pad_maximum_fusion
  460.3 4.3 copy.95
  464.6 77.4 %all-reduce.21.cloned.1.call-done = f32[5,9216]{1,0:T(8,128)} async-done(((f32[5,9216]{1,0:T(8,128)}), f32[5,9216]{1,0:T(8,128)}) %all-reduce.21.cloned.1.call-update) | async-done | bytes 184336 | tf_op jit(solution)/shard_map/psum | solution.py:198
  541.9 1.7 copy.143
  (101 shorter events, 11.0 us)
Async XLA Ops:
  7.2 130.8 %all-gather.7.cloned.1.call-start = ((), (), s32[]{:S(2)}) async-start(), calls=%async_computation.1 | async-start | bytes 18874368 | tf_op jit(solution)/shard_map/all_gather | solution.py:26
  8.2 13.1 %collective-permute-start = (bf16[1,3,9216]{2,1,0:T(4,128)(2,1)S(1)}, bf16[1,3,9216]{2,1,0:T(4,128)(2,1)S(1)}, u32[]{:S(2)}, u32[]{:S(2)}) collective-permute-start(bf16[1,3,9216]{2,1,0:T(4,128)(2,1)S(1)} %slice.83), channel_id=1, source_target_pairs={{0,4},{4,8},{8,12},{12,16},{16,20},{20,24},{24,28},{1,5},{5,9},{9,... | collective-permute-start | bytes 165896 | tf_op jit(solution)/shard_map/ppermute | solution.py:18
  11.7 15.0 %copy-start.7 = (f32[1,9216]{1,0:T(1,128)}, f32[1,9216]{1,0:T(1,128)S(1)}, u32[]{:S(2)}) copy-start(f32[1,9216]{1,0:T(1,128)S(1)} %get-tuple-element.549) | copy-start | bytes 110596
  11.7 15.0 %copy-start.9 = (f32[1,9216]{1,0:T(1,128)}, f32[1,9216]{1,0:T(1,128)S(1)}, u32[]{:S(2)}) copy-start(f32[1,9216]{1,0:T(1,128)S(1)} %get-tuple-element.550) | copy-start | bytes 110596
  11.7 15.0 %copy-start.11 = (f32[1,9216]{1,0:T(1,128)}, f32[1,9216]{1,0:T(1,128)S(1)}, u32[]{:S(2)}) copy-start(f32[1,9216]{1,0:T(1,128)S(1)} %get-tuple-element.551) | copy-start | bytes 110596
  26.7 12.4 %copy-start.3 = (f32[131,9216]{0,1:T(8,128)}, f32[131,9216]{0,1:T(8,128)S(1)}, u32[]{:S(2)}) copy-start(f32[131,9216]{0,1:T(8,128)S(1)} %maximum_convert_fusion) | copy-start | bytes 14487556
  39.1 2.1 copy-start.5
  46.3 253.2 %all-gather.5.cloned.1.call-start = ((), (), s32[]{:S(2)}) async-start(), calls=%async_computation | async-start | bytes 18874368 | tf_op jit(solution)/shard_map/all_gather | solution.py:26
  55.6 9.8 %copy-start.17 = (f32[128,128]{1,0:T(8,128)}, f32[128,128]{1,0:T(8,128)S(1)}, u32[]{:S(2)}) copy-start(f32[128,128]{1,0:T(8,128)S(1)} %copy.71) | copy-start | bytes 196612
  55.7 9.7 %copy-start.19 = (f32[1,128,128]{2,1,0:T(8,128)}, f32[1,128,128]{2,1,0:T(8,128)S(1)}, u32[]{:S(2)}) copy-start(f32[1,128,128]{2,1,0:T(8,128)S(1)} %copy.70) | copy-start | bytes 196612
  55.9 9.5 %copy-start.20 = (pred[128,128]{1,0:T(8,128)(4,1)}, pred[128,128]{1,0:T(8,128)(4,1)S(1)}, u32[]{:S(2)}) copy-start(pred[128,128]{1,0:T(8,128)(4,1)S(1)} %iota_compare_fusion) | copy-start | bytes 49156
  56.0 137.3 %copy-start.24 = (f32[128]{0:T(128)}, f32[128]{0:T(128)S(1)}, u32[]{:S(2)}) copy-start(f32[128]{0:T(128)S(1)} %slice_bitcast_fusion.5) | copy-start | bytes 1540
  57.2 8.2 %copy-start.13 = (f32[4,128,128]{2,1,0:T(8,128)}, f32[4,128,128]{2,1,0:T(8,128)S(1)}, u32[]{:S(2)}) copy-start(f32[4,128,128]{2,1,0:T(8,128)S(1)} %fusion.120) | copy-start | bytes 786436
  178.9 5.5 copy-start.22
  184.4 8.7 %copy-start.6 = (f32[4,32,64,128]{3,2,1,0:T(8,128)}, f32[4,32,64,128]{3,2,1,0:T(8,128)S(1)}, u32[]{:S(2)}) copy-start(f32[4,32,64,128]{3,2,1,0:T(8,128)S(1)} %fusion.121) | copy-start | bytes 12582916
  203.5 1.9 copy-start.4
  210.3 5.0 copy-start.18
  210.3 331.6 %all-reduce.21.cloned.1.call-start = ((), (), s32[]{:S(2)}) async-start(), calls=%async_computation.2 | async-start | bytes 589824 | tf_op jit(solution)/shard_map/psum | solution.py:198
  244.1 5.9 %copy-start = (f32[128,64,128]{2,1,0:T(8,128)S(1)}, f32[128,64,128]{2,1,0:T(8,128)}, u32[]{:S(2)}) copy-start(f32[128,64,128]{2,1,0:T(8,128)} %get-tuple-element.485) | copy-start | bytes 12582916
  301.9 9.9 %copy-start.2 = (f32[128,64,128]{2,1,0:T(8,128)S(1)}, f32[128,64,128]{2,1,0:T(8,128)}, u32[]{:S(2)}) copy-start(f32[128,64,128]{2,1,0:T(8,128)} %get-tuple-element.484) | copy-start | bytes 12582916
  311.9 4.2 copy-start.1
  316.1 3.5 copy-start.14
  316.1 3.5 copy-start.15
  316.1 3.5 copy-start.16
  328.6 21.1 %copy-start.8 = (f32[1,9216]{1,0:T(1,128)S(1)}, f32[1,9216]{1,0:T(1,128)}, u32[]{:S(2)}) copy-start(f32[1,9216]{1,0:T(1,128)} %copy-done.7) | copy-start | bytes 110596
  328.6 21.1 %copy-start.10 = (f32[1,9216]{1,0:T(1,128)S(1)}, f32[1,9216]{1,0:T(1,128)}, u32[]{:S(2)}) copy-start(f32[1,9216]{1,0:T(1,128)} %copy-done.9) | copy-start | bytes 110596
  328.6 21.1 %copy-start.12 = (f32[1,9216]{1,0:T(1,128)S(1)}, f32[1,9216]{1,0:T(1,128)}, u32[]{:S(2)}) copy-start(f32[1,9216]{1,0:T(1,128)} %copy-done.11) | copy-start | bytes 110596
  366.7 5.9 %copy-start.25 = (f32[128]{0:T(128)S(1)}, f32[128]{0:T(128)}, u32[]{:S(2)}) copy-start(f32[128]{0:T(128)} %get-tuple-element.552) | copy-start | bytes 1540
  366.7 6.6 %copy-start.21 = (f32[128]{0:T(128)S(1)}, f32[128]{0:T(128)}, u32[]{:S(2)}) copy-start(f32[128]{0:T(128)} %reduce_sum.319) | copy-start | bytes 1540
  366.7 6.6 %copy-start.23 = (f32[128]{0:T(128)S(1)}, f32[128]{0:T(128)}, u32[]{:S(2)}) copy-start(f32[128]{0:T(128)} %get-tuple-element.529) | copy-start | bytes 1540
  369.6 83.0 %collective-permute-start.1 = (bf16[1,3,9216]{2,1,0:T(4,128)(2,1)S(1)}, bf16[1,3,9216]{2,1,0:T(4,128)(2,1)S(1)}, u32[]{:S(2)}, u32[]{:S(2)}) collective-permute-start(bf16[1,3,9216]{2,1,0:T(4,128)(2,1)S(1)} %copy.84), channel_id=1, source_target_pairs={{4,0},{8,4},{12,8},{16,12},{20,16},{24,20},{28,24},{5,1},{9,5},{13... | collective-permute-start | bytes 165896 | tf_op jit(solution)/shard_map/ppermute | solution.py:18
Sparse Core Ops, SparseCore 0:
  46.4 91.4 all-gather.6
  210.5 88.9 all-gather.4
  372.7 169.2 all-reduce.20
where the time goes:
time: 558 us; the launch traced here: 551 us
  waiting for transfers between devices  189 us (34%)
  other arithmetic  125 us (22%)
  blocking collectives  88.3 us (16%)
  matrix products  86.4 us (15%)
  local copies, waits for them, and re-layouts  43.4 us (8%)
  between operations  14.8 us (3%)
    all_gather x2, waiting for transfers between devices, entering_2(): lax.all_gather(a.astype(kind), axis)  112 us
    psum x1, blocking collectives, shards(): total_conv, total_head = lax.psum((grad_conv, grad_head), ('ctx', 'fsdp'))  79.4 us
    psum x1, waiting for transfers between devices, shards(): total_conv, total_head = lax.psum((grad_conv, grad_head), ('ctx', 'fsdp'))  77.4 us
    add x7, other arithmetic, combine_carry(): later_pair[0][:, None, None] * earlier_pair[1] + later_pair[1]  38 us
    dot_general x2, matrix products, advance(): jnp.einsum('gkts,sgkp->tgkp', weights, x_grouped, precision=exact_prec)  21.6 us
    reduce_sum x1, other arithmetic, prepare(): conv_params[offset][None, :] * extended[offset:offset + row_count]  21 us
    dot_general x3, matrix products, end_state(): jnp.einsum('sgkp,sgn->gkpn', weighted, b_groups, precision=exact_prec)  20.1 us
    unnamed x59, local copies, waits for them, and re-layouts  19.2 us
  transfers between devices with their start and end apart: 5, of which 3 were waited for; matrix products, arithmetic and copies ran while one was open for 15% of the time, Pallas kernels for 0%

commit v1 on v0

--- a/solution.py
+++ b/solution.py
@@ -195,7 +195,7 @@
         [own_rows[: row_count - rim_rows], own_rows[row_count - rim_rows :] + returned_rim[0]],
         axis=0,
     )
-    total_conv, total_head = lax.psum((grad_conv, grad_head), ("ctx", "fsdp"))
+    total_conv, total_head = lax.psum(lax.psum((grad_conv, grad_head), "fsdp"), "ctx")
     return (own_rows[None].astype(jnp.bfloat16), grad_dt[None], total_conv, total_head)
 
 

time: 558 us -> 523 us (0.937)
  waiting for transfers between devices: 189 us -> 168 us
  blocking collectives: 88.3 us -> 71.6 us
    psum x1 -> x2, waiting for transfers between devices: 77.4 us -> 55.8 us  [the longest x1 47.9 us: shards(): lax.psum(lax.psum((grad_conv, grad_head), 'fsdp'), 'ctx')]
    psum x1 -> x2, blocking collectives: 79.4 us -> 62.7 us  [the longest x1 53.8 us: shards(): lax.psum(lax.psum((grad_conv, grad_head), 'fsdp'), 'ctx')]
  transfers between devices with their start and end apart: 5 -> 6, of which waited for: 3 -> 4; matrix products, arithmetic and copies ran while one was open for 15% -> 17% of each run, Pallas kernels for 0% -> 0%
where the time goes in v1:
time: 523 us; the launch traced here: 515 us
  waiting for transfers between devices  168 us (32%)
  other arithmetic  127 us (24%)
  matrix products  86.4 us (17%)
  blocking collectives  71.6 us (14%)
  local copies, waits for them, and re-layouts  43.4 us (8%)
  between operations  14.8 us (3%)
    all_gather x2, waiting for transfers between devices, entering_2(): lax.all_gather(a.astype(kind), axis)  112 us
    psum x1, blocking collectives, shards(): lax.psum(lax.psum((grad_conv, grad_head), 'fsdp'), 'ctx')  53.8 us
    psum x1, waiting for transfers between devices, shards(): lax.psum(lax.psum((grad_conv, grad_head), 'fsdp'), 'ctx')  47.9 us
    add x7, other arithmetic, combine_carry(): later_pair[0][:, None, None] * earlier_pair[1] + later_pair[1]  38 us
    dot_general x2, matrix products, advance(): jnp.einsum('gkts,sgkp->tgkp', weights, x_grouped, precision=exact_prec)  21.6 us
    reduce_sum x1, other arithmetic, prepare(): conv_params[offset][None, :] * extended[offset:offset + row_count]  21 us
    dot_general x3, matrix products, end_state(): jnp.einsum('sgkp,sgn->gkpn', weighted, b_groups, precision=exact_prec)  20.1 us
    unnamed x59, local copies, waits for them, and re-layouts  19.2 us
  transfers between devices with their start and end apart: 6, of which 4 were waited for; matrix products, arithmetic and copies ran while one was open for 17% of the time, Pallas kernels for 0%

profile of v1, /device:TPU:8, one launch (start us, length us, event | category | flops | bytes accessed | tf_op | source)
XLA Modules:
  0.0 514.6 jit_solution(10715148402526287706)
XLA Ops:
  7.2 1.0 slice.83
  8.2 1.7 collective-permute-start
  9.9 1.8 fusion.119
  13.7 4.3 copy.69
  17.9 3.2 copy.65
  21.3 2.0 copy.68
  23.3 3.4 maximum_convert_fusion
  26.7 12.4 %fusion.11 = (f32[128,9216]{0,1:T(8,128)S(1)}, f32[128,9216]{0,1:T(8,128)}) fusion(f32[131,9216]{0,1:T(8,128)S(1)} %maximum_convert_fusion, f32[9216]{0:T(1024)S(1)} %bitcast.354, f32[9216]{0:T(1024)S(1)} %bitcast.356, f32[9216]{0:T(1024)S(1)} %bitcast.358, f32[9216]{0:T(1024)S(1)} %bitcast.352, f32[9216]{0:T(1024)S(1)} %bitcast.365), kind=kLoop, calls=%fused_computation.34 | loop fusion | flops 14155776 | bytes 28495872 | tf_op jit(solution)/shard_map/jvp(jit(silu))/mul | solution.py:59
  39.1 2.1 copy-done.5
  41.3 5.0 fusion.53
  46.4 8.9 %all-gather.1 = bf16[8,1,128]{2,1,0:T(2,128)(2,1)S(1)} all-gather(bf16[1,1,128]{2,1,0:T(2,128)(2,1)S(1)} %convert_bitcast_fusion.1), channel_id=2, replica_groups=mesh['ctx'=8,'fsdp'=4] {'ctx'}, dimensions={0}, use_global_device_ids=true | all-gather | bytes 2304 | tf_op jit(solution)/shard_map/all_gather | solution.py:26
  57.2 8.2 %fusion.1 = f32[4,32,128,64]{2,3,1,0:T(8,128)} fusion(bf16[4,32,64,128]{3,2,1,0:T(8,128)(2,1)S(1)} %bitcast.325, f32[4,128,128]{2,1,0:T(8,128)S(1)} %fusion.120, f32[4,32,128]{2,1,0:T(8,128)S(1)} %bitcast.371, f32[4,32,128]{2,1,0:T(8,128)S(1)} %bitcast.373, pred[128,128]{1,0:T(8,128)(4,1)S(1)} %iota_compare_fusion), kind=kOutput, calls=%fused_computation.9 | convolution fusion | flops 1623195648 | bytes 6701056 | tf_op jit(solution)/shard_map/transpose(jvp())/while/body/eval_jaxpr/gkts,sgkp->tgkp/dot_general | solution.py:89
  65.4 72.6 %all-gather.7.cloned.1.call-done = bf16[8,128,64,128]{3,2,1,0:T(8,128)(2,1)} async-done(((bf16[1,128,64,128]{3,2,1,0:T(8,128)(2,1)}), bf16[8,128,64,128]{3,2,1,0:T(8,128)(2,1)}) %all-gather.7.cloned.1.call-update) | async-done | bytes 16777232 | tf_op jit(solution)/shard_map/all_gather | solution.py:26
  138.0 2.6 broadcast.354.clone
  140.6 38.3 %while.21 = (s32[]{:T(128)}, f32[128,64,128]{2,1,0:T(8,128)}, s32[]{:T(128)}, bf16[8,128]{1,0:T(8,128)(2,1)S(1)}, bf16[8,128,64,128]{3,2,1,0:T(8,128)(2,1)}, /*index=5*/s32[]{:T(128)}, s32[]{:T(128)}, s32[]{:T(128)}, s32[]{:T(128)}) while((s32[]{:T(128)}, f32[128,64,128]{2,1,0:T(8,128)}, s32[]{:T(128)}, bf16[8,128]{1,0:T(8,128)(2,1)S(1)}, ...), condition=%wide.region_7.8_spmd, body=%wide.region_6.7_spmd.sunk | while | flops 3145862 | bytes 10487195 | solution.py:41
  140.6 5.4 %convert_add_fusion.6 = f32[128,64,128]{2,1,0:T(8,128)} fusion(f32[128,64,128]{2,1,0:T(8,128)} %get-tuple-element.645, bf16[8,128,64,128]{3,2,1,0:T(8,128)(2,1)} %get-tuple-element.657, s32[]{:T(128)S(6)} %select_n.218, f32[128]{0:T(128)S(1)} %bitcast_convert_fusion.5), kind=kLoop, calls=%fused_computation.2.clone.1 | loop fusion | flops 3145728 | bytes 10486276 | tf_op jit(solution)/shard_map/while/body/add | solution.py:151
  146.0 5.4 %convert_add_fusion.6 = f32[128,64,128]{2,1,0:T(8,128)} fusion(f32[128,64,128]{2,1,0:T(8,128)} %get-tuple-element.645, bf16[8,128,64,128]{3,2,1,0:T(8,128)(2,1)} %get-tuple-element.657, s32[]{:T(128)S(6)} %select_n.218, f32[128]{0:T(128)S(1)} %bitcast_convert_fusion.5), kind=kLoop, calls=%fused_computation.2.clone.1 | loop fusion | flops 3145728 | bytes 10486276 | tf_op jit(solution)/shard_map/while/body/add | solution.py:151
  151.5 5.4 %convert_add_fusion.6 = f32[128,64,128]{2,1,0:T(8,128)} fusion(f32[128,64,128]{2,1,0:T(8,128)} %get-tuple-element.645, bf16[8,128,64,128]{3,2,1,0:T(8,128)(2,1)} %get-tuple-element.657, s32[]{:T(128)S(6)} %select_n.218, f32[128]{0:T(128)S(1)} %bitcast_convert_fusion.5), kind=kLoop, calls=%fused_computation.2.clone.1 | loop fusion | flops 3145728 | bytes 10486276 | tf_op jit(solution)/shard_map/while/body/add | solution.py:151
  156.9 5.4 %convert_add_fusion.6 = f32[128,64,128]{2,1,0:T(8,128)} fusion(f32[128,64,128]{2,1,0:T(8,128)} %get-tuple-element.645, bf16[8,128,64,128]{3,2,1,0:T(8,128)(2,1)} %get-tuple-element.657, s32[]{:T(128)S(6)} %select_n.218, f32[128]{0:T(128)S(1)} %bitcast_convert_fusion.5), kind=kLoop, calls=%fused_computation.2.clone.1 | loop fusion | flops 3145728 | bytes 10486276 | tf_op jit(solution)/shard_map/while/body/add | solution.py:151
  162.4 5.4 %convert_add_fusion.6 = f32[128,64,128]{2,1,0:T(8,128)} fusion(f32[128,64,128]{2,1,0:T(8,128)} %get-tuple-element.645, bf16[8,128,64,128]{3,2,1,0:T(8,128)(2,1)} %get-tuple-element.657, s32[]{:T(128)S(6)} %select_n.218, f32[128]{0:T(128)S(1)} %bitcast_convert_fusion.5), kind=kLoop, calls=%fused_computation.2.clone.1 | loop fusion | flops 3145728 | bytes 10486276 | tf_op jit(solution)/shard_map/while/body/add | solution.py:151
  167.8 5.4 %convert_add_fusion.6 = f32[128,64,128]{2,1,0:T(8,128)} fusion(f32[128,64,128]{2,1,0:T(8,128)} %get-tuple-element.645, bf16[8,128,64,128]{3,2,1,0:T(8,128)(2,1)} %get-tuple-element.657, s32[]{:T(128)S(6)} %select_n.218, f32[128]{0:T(128)S(1)} %bitcast_convert_fusion.5), kind=kLoop, calls=%fused_computation.2.clone.1 | loop fusion | flops 3145728 | bytes 10486276 | tf_op jit(solution)/shard_map/while/body/add | solution.py:151
  173.2 5.4 %convert_add_fusion.6 = f32[128,64,128]{2,1,0:T(8,128)} fusion(f32[128,64,128]{2,1,0:T(8,128)} %get-tuple-element.645, bf16[8,128,64,128]{3,2,1,0:T(8,128)(2,1)} %get-tuple-element.657, s32[]{:T(128)S(6)} %select_n.218, f32[128]{0:T(128)S(1)} %bitcast_convert_fusion.5), kind=kLoop, calls=%fused_computation.2.clone.1 | loop fusion | flops 3145728 | bytes 10486276 | tf_op jit(solution)/shard_map/while/body/add | solution.py:151
  178.9 5.5 %fusion.121 = f32[4,32,64,128]{3,2,1,0:T(8,128)S(1)} fusion(f32[4,32,64,128]{3,2,1,0:T(8,128)} %bitcast.316, f32[128,4,128,1]{0,2,3,1:T(8,128)S(1)} %bitcast.335), kind=kOutput, calls=%fused_computation.179 | convolution fusion | flops 1610612736 | bytes 8650752 | tf_op jit(solution)/shard_map/transpose(jvp(sgkp,sgn->gkpn))/dot_general | solution.py:118
  184.4 8.7 %fusion.23 = (f32[128,4,32]{0,2,1:T(8,128)S(1)}, f32[128,4,32]{0,2,1:T(8,128)S(1)}, f32[4,32,64,128]{3,2,1,0:T(8,128)}) fusion(f32[128,9216]{0,1:T(8,128)} %copy-done.5, f32[4,32,64,128]{3,2,1,0:T(8,128)S(1)} %fusion.121, f32[128,4,128,1]{0,2,3,1:T(8,128)S(1)} %bitcast.336), kind=kOutput, calls=%fused_computation.50 | convolution fusion | flops 1614774272 | bytes 12976128 | tf_op jit(solution)/shard_map/transpose(jvp())/while/body/eval_jaxpr/sgkp,sgn->gkpn/dot_general | solution.py:100
  194.2 9.4 %fusion.16 = (f32[8192]{0:T(1024)}, f32[128,8192]{0,1:T(8,128)S(1)}, f32[128,8192]{0,1:T(8,128)}) fusion(bf16[1,128,8192]{1,2,0:T(8,128)(2,1)S(1)} %copy.65, f32[128,9216]{0,1:T(8,128)} %copy-done.5, f32[4,32,64,128]{3,2,1,0:T(8,128)} %copy-done.6, f32[128,128]{0,1:T(8,128)S(1)} %copy.73, f32[4,32,128,64]{2,3,1,0:T(8,128)} %fusion.1, ...), kind=kLoop, calls=%fused_computation.39 | loop fusion | flops 9428992 | bytes 27459584 | tf_op jit(solution)/shard_map/transpose(jvp())/reduce_sum | solution.py:108
  203.5 1.9 copy-done.4
  205.4 4.9 fusion.50
  210.8 3.8 fusion.21
  215.3 13.4 %fusion.37 = (f32[4,32,128]{2,1,0:T(8,128)}, f32[4,32,128]{2,1,0:T(8,128)}, f32[4,32,128]{2,1,0:T(8,128)}, f32[4,128,128]{2,1,0:T(8,128)S(1)}) fusion(f32[4,32,128]{2,1,0:T(8,128)S(1)} %bitcast.372, f32[4,32,128]{2,1,0:T(8,128)} %bitcast.374, f32[4,128,128]{2,1,0:T(8,128)} %copy-done.13, pred[128,128]{1,0:T(8,128)(4,1)} %copy-done.20, ...), kind=kOutput, calls=%fused_computation.65 | convolution fusion | flops 1646149632 | bytes 7159808 | tf_op jit(solution)/shard_map/transpose(jvp())/while/body/eval_jaxpr/gkts,sgkp->tgkp/dot_general | solution.py:89
  228.7 1.6 copy.92
  231.9 1.6 copy.87
  234.3 1.2 negate_bitcast_fusion
  235.4 1.6 fusion.94
  237.1 2.6 reduce_window_sum.53
  239.6 1.2 pad_add_fusion.2
  240.9 2.6 reduce_window_sum.54
  244.1 5.9 %fusion.68 = f32[128,4,128]{0,2,1:T(8,128)S(1)} fusion(f32[128,4,32,64]{0,3,2,1:T(8,128)} %bitcast.322, f32[128,4,32]{0,2,1:T(8,128)S(1)} %bitcast.351), kind=kOutput, calls=%fused_computation.95 | convolution fusion | flops 1611661312 | bytes 4521984 | tf_op jit(solution)/shard_map/transpose(jvp())/while/body/eval_jaxpr/sgkp,sgn->gkpn/dot_general | solution.py:100
  250.0 9.7 %fusion.54 = f32[128,4,128]{0,2,1:T(8,128)S(1)} fusion(f32[4,32,64,128]{3,2,1,0:T(8,128)S(1)} %bitcast.317, f32[128,4,32,64]{0,3,2,1:T(8,128)} %bitcast.323, f32[128,4,32]{0,2,1:T(8,128)S(1)} %bitcast.346), kind=kOutput, calls=%fused_computation.87 | convolution fusion | flops 1611661312 | bytes 8716288 | tf_op jit(solution)/shard_map/transpose(jvp(sgkp,sgn->gkpn))/dot_general | solution.py:118
  260.1 39.4 %all-gather.5.cloned.1.call-done = bf16[8,128,64,128]{3,2,1,0:T(8,128)(2,1)} async-done(((bf16[1,128,64,128]{3,2,1,0:T(8,128)(2,1)}), bf16[8,128,64,128]{3,2,1,0:T(8,128)(2,1)}) %all-gather.5.cloned.1.call-update) | async-done | bytes 16777232 | tf_op jit(solution)/shard_map/all_gather | solution.py:26
  299.5 2.5 broadcast.354
  301.9 9.9 %fusion.57 = f32[4,128,128]{1,2,0:T(8,128)} fusion(f32[4,32,64,128]{3,2,1,0:T(8,128)} %bitcast.318, bf16[128,4,32,64]{0,3,2,1:T(8,128)(2,1)S(1)} %bitcast.328, f32[128,4,32]{0,2,1:T(8,128)S(1)} %bitcast.350), kind=kOutput, calls=%fused_computation.88 | convolution fusion | flops 1612709888 | bytes 6619136 | tf_op jit(solution)/shard_map/transpose(jvp(tgn,gkpn->tgkp))/dot_general | solution.py:126
  311.9 4.2 fusion.20
  316.1 1.5 multiply_reduce_fusion.5
  318.4 1.1 reduce_window_sum.55
  319.6 1.9 fusion.112
  321.5 0.9 copy.67
  322.4 4.6 fusion.63
  327.0 1.6 fusion.62
  328.6 21.0 %multiply_reduce_fusion.4 = (f32[9216]{0:T(1024)S(1)}, f32[9216]{0:T(1024)S(1)}, f32[9216]{0:T(1024)S(1)}, f32[9216]{0:T(1024)S(1)}, f32[9216]{0:T(1024)S(1)}, /*index=5*/f32[128,9216]{0,1:T(8,128)S(1)}) fusion(f32[131,9216]{0,1:T(8,128)} %copy-done.3, f32[128,9216]{0,1:T(8,128)} %get-tuple-element.537, f32[128,8192]{0,1:T(8,128)} %get-tuple-element.546, ...), kind=kLoop, calls=%fused_computation.32 | loop fusion | flops 23546880 | bytes 33214464 | tf_op jit(solution)/shard_map/transpose(jvp())/reduce_sum | solution.py:58
  349.7 6.1 %broadcast_multiply_fusion.3 = (f32[128,9216]{0,1:T(8,128)S(1)}, f32[128,9216]{0,1:T(8,128)S(1)}, f32[128,9216]{0,1:T(8,128)S(1)}, f32[128,9216]{0,1:T(8,128)S(1)}) fusion(f32[128,9216]{0,1:T(8,128)S(1)} %get-tuple-element.531, f32[9216]{0:T(1024)S(1)} %bitcast.355, f32[9216]{0:T(1024)S(1)} %bitcast.353, f32[9216]{0:T(1024)S(1)} %bitcast.359, ...), kind=kLoop, calls=%fused_computation.73 | loop fusion | flops 4718592 | bytes 23740416 | tf_op jit(solution)/shard_map/transpose(jvp())/mul | solution.py:58
  355.8 9.4 %fusion.117 = (bf16[131,9216]{0,1:T(8,128)(2,1)S(1)}, f32[131,9216]{0,1:T(8,128)}) fusion(f32[128,9216]{0,1:T(8,128)S(1)} %get-tuple-element.541, f32[128,9216]{0,1:T(8,128)S(1)} %get-tuple-element.542, f32[128,9216]{0,1:T(8,128)S(1)} %get-tuple-element.543, f32[128,9216]{0,1:T(8,128)S(1)} %get-tuple-element.540), kind=kLoop, calls=%fused_computation.175 | loop fusion | flops 4829184 | bytes 26118144 | tf_op jit(solution)/shard_map/convert.12
  365.2 1.5 slice_bitcast_fusion
  367.5 2.1 copy.84
  369.6 1.3 collective-permute-start.1
  371.6 0.9 pad_add_fusion.1
  373.3 8.9 %psum.30 = f32[3,128]{1,0:T(4,128)S(1)} all-reduce(f32[3,128]{1,0:T(4,128)S(1)} %pad_add_fusion.3), channel_id=1, replica_groups=mesh['ctx'=8,'fsdp'=4] {'fsdp'}, use_global_device_ids=true, to_apply=%region_32.33 | all-reduce | flops 384 | bytes 3072 | tf_op jit(solution)/shard_map/psum | solution.py:198
  382.2 53.8 %psum.31 = f32[3,128]{1,0:T(4,128)} all-reduce(f32[3,128]{1,0:T(4,128)S(1)} %psum.30), channel_id=1, replica_groups=mesh['ctx'=8,'fsdp'=4] {'ctx'}, use_global_device_ids=true, to_apply=%region_33.34 | all-reduce | flops 384 | bytes 3072 | tf_op jit(solution)/shard_map/psum | solution.py:198
  436.0 1.9 copy.85
  437.9 4.3 fusion.38
  442.2 7.8 %all-reduce.22.cloned.1.call-done = f32[5,9216]{1,0:T(8,128)} async-done(((f32[5,9216]{1,0:T(8,128)}), f32[5,9216]{1,0:T(8,128)}) %all-reduce.22.cloned.1.call-update) | async-done | bytes 184336 | tf_op jit(solution)/shard_map/psum | solution.py:198
  450.1 3.6 pad_maximum_fusion
  453.7 4.3 copy.95
  458.0 47.9 %all-reduce.24.cloned.1.call-done = f32[5,9216]{1,0:T(8,128)} async-done(((f32[5,9216]{1,0:T(8,128)}), f32[5,9216]{1,0:T(8,128)}) %all-reduce.24.cloned.1.call-update) | async-done | bytes 184336 | tf_op jit(solution)/shard_map/psum | solution.py:198
  506.0 1.7 copy.144
  (105 shorter events, 12.8 us)
Async XLA Ops:
  7.2 130.8 %all-gather.7.cloned.1.call-start = ((), (), s32[]{:S(2)}) async-start(), calls=%async_computation.1 | async-start | bytes 18874368 | tf_op jit(solution)/shard_map/all_gather | solution.py:26
  8.2 13.1 %collective-permute-start = (bf16[1,3,9216]{2,1,0:T(4,128)(2,1)S(1)}, bf16[1,3,9216]{2,1,0:T(4,128)(2,1)S(1)}, u32[]{:S(2)}, u32[]{:S(2)}) collective-permute-start(bf16[1,3,9216]{2,1,0:T(4,128)(2,1)S(1)} %slice.83), channel_id=1, source_target_pairs={{0,4},{4,8},{8,12},{12,16},{16,20},{20,24},{24,28},{1,5},{5,9},{9,... | collective-permute-start | bytes 165896 | tf_op jit(solution)/shard_map/ppermute | solution.py:18
  11.7 15.0 %copy-start.7 = (f32[1,9216]{1,0:T(1,128)}, f32[1,9216]{1,0:T(1,128)S(1)}, u32[]{:S(2)}) copy-start(f32[1,9216]{1,0:T(1,128)S(1)} %get-tuple-element.549) | copy-start | bytes 110596
  11.7 15.0 %copy-start.9 = (f32[1,9216]{1,0:T(1,128)}, f32[1,9216]{1,0:T(1,128)S(1)}, u32[]{:S(2)}) copy-start(f32[1,9216]{1,0:T(1,128)S(1)} %get-tuple-element.550) | copy-start | bytes 110596
  11.7 15.0 %copy-start.11 = (f32[1,9216]{1,0:T(1,128)}, f32[1,9216]{1,0:T(1,128)S(1)}, u32[]{:S(2)}) copy-start(f32[1,9216]{1,0:T(1,128)S(1)} %get-tuple-element.551) | copy-start | bytes 110596
  26.7 12.4 %copy-start.3 = (f32[131,9216]{0,1:T(8,128)}, f32[131,9216]{0,1:T(8,128)S(1)}, u32[]{:S(2)}) copy-start(f32[131,9216]{0,1:T(8,128)S(1)} %maximum_convert_fusion) | copy-start | bytes 14487556
  39.1 2.1 copy-start.5
  46.3 253.2 %all-gather.5.cloned.1.call-start = ((), (), s32[]{:S(2)}) async-start(), calls=%async_computation | async-start | bytes 18874368 | tf_op jit(solution)/shard_map/all_gather | solution.py:26
  55.6 9.8 %copy-start.17 = (f32[128,128]{1,0:T(8,128)}, f32[128,128]{1,0:T(8,128)S(1)}, u32[]{:S(2)}) copy-start(f32[128,128]{1,0:T(8,128)S(1)} %copy.71) | copy-start | bytes 196612
  55.7 9.7 %copy-start.19 = (f32[1,128,128]{2,1,0:T(8,128)}, f32[1,128,128]{2,1,0:T(8,128)S(1)}, u32[]{:S(2)}) copy-start(f32[1,128,128]{2,1,0:T(8,128)S(1)} %copy.70) | copy-start | bytes 196612
  55.9 9.5 %copy-start.20 = (pred[128,128]{1,0:T(8,128)(4,1)}, pred[128,128]{1,0:T(8,128)(4,1)S(1)}, u32[]{:S(2)}) copy-start(pred[128,128]{1,0:T(8,128)(4,1)S(1)} %iota_compare_fusion) | copy-start | bytes 49156
  56.0 137.3 %copy-start.24 = (f32[128]{0:T(128)}, f32[128]{0:T(128)S(1)}, u32[]{:S(2)}) copy-start(f32[128]{0:T(128)S(1)} %slice_bitcast_fusion.5) | copy-start | bytes 1540
  57.2 8.2 %copy-start.13 = (f32[4,128,128]{2,1,0:T(8,128)}, f32[4,128,128]{2,1,0:T(8,128)S(1)}, u32[]{:S(2)}) copy-start(f32[4,128,128]{2,1,0:T(8,128)S(1)} %fusion.120) | copy-start | bytes 786436
  178.9 5.5 %copy-start.22 = (bf16[8,128]{1,0:T(8,128)(2,1)}, bf16[8,128]{1,0:T(8,128)(2,1)S(1)}, u32[]{:S(2)}) copy-start(bf16[8,128]{1,0:T(8,128)(2,1)S(1)} %get-tuple-element.710) | copy-start | bytes 6148
  184.4 8.7 %copy-start.6 = (f32[4,32,64,128]{3,2,1,0:T(8,128)}, f32[4,32,64,128]{3,2,1,0:T(8,128)S(1)}, u32[]{:S(2)}) copy-start(f32[4,32,64,128]{3,2,1,0:T(8,128)S(1)} %fusion.121) | copy-start | bytes 12582916
  203.5 1.9 copy-start.4
  210.3 5.0 copy-start.18
  210.3 239.7 %all-reduce.22.cloned.1.call-start = ((), (), s32[]{:S(2)}) async-start(), calls=%async_computation.2 | async-start | bytes 589824 | tf_op jit(solution)/shard_map/psum | solution.py:198
  244.1 5.9 %copy-start = (f32[128,64,128]{2,1,0:T(8,128)S(1)}, f32[128,64,128]{2,1,0:T(8,128)}, u32[]{:S(2)}) copy-start(f32[128,64,128]{2,1,0:T(8,128)} %get-tuple-element.485) | copy-start | bytes 12582916
  301.9 9.9 %copy-start.2 = (f32[128,64,128]{2,1,0:T(8,128)S(1)}, f32[128,64,128]{2,1,0:T(8,128)}, u32[]{:S(2)}) copy-start(f32[128,64,128]{2,1,0:T(8,128)} %get-tuple-element.484) | copy-start | bytes 12582916
  311.9 4.2 copy-start.1
  316.1 3.5 copy-start.14
  316.1 3.5 copy-start.15
  316.1 3.5 copy-start.16
  328.6 21.1 %copy-start.8 = (f32[1,9216]{1,0:T(1,128)S(1)}, f32[1,9216]{1,0:T(1,128)}, u32[]{:S(2)}) copy-start(f32[1,9216]{1,0:T(1,128)} %copy-done.7) | copy-start | bytes 110596
  328.6 21.1 %copy-start.10 = (f32[1,9216]{1,0:T(1,128)S(1)}, f32[1,9216]{1,0:T(1,128)}, u32[]{:S(2)}) copy-start(f32[1,9216]{1,0:T(1,128)} %copy-done.9) | copy-start | bytes 110596
  328.6 21.1 %copy-start.12 = (f32[1,9216]{1,0:T(1,128)S(1)}, f32[1,9216]{1,0:T(1,128)}, u32[]{:S(2)}) copy-start(f32[1,9216]{1,0:T(1,128)} %copy-done.11) | copy-start | bytes 110596
  366.7 5.9 %copy-start.25 = (f32[128]{0:T(128)S(1)}, f32[128]{0:T(128)}, u32[]{:S(2)}) copy-start(f32[128]{0:T(128)} %get-tuple-element.552) | copy-start | bytes 1540
  366.7 6.6 %copy-start.21 = (f32[128]{0:T(128)S(1)}, f32[128]{0:T(128)}, u32[]{:S(2)}) copy-start(f32[128]{0:T(128)} %reduce_sum.319) | copy-start | bytes 1540
  366.7 6.6 %copy-start.23 = (f32[128]{0:T(128)S(1)}, f32[128]{0:T(128)}, u32[]{:S(2)}) copy-start(f32[128]{0:T(128)} %get-tuple-element.529) | copy-start | bytes 1540
  369.6 66.4 %collective-permute-start.1 = (bf16[1,3,9216]{2,1,0:T(4,128)(2,1)S(1)}, bf16[1,3,9216]{2,1,0:T(4,128)(2,1)S(1)}, u32[]{:S(2)}, u32[]{:S(2)}) collective-permute-start(bf16[1,3,9216]{2,1,0:T(4,128)(2,1)S(1)} %copy.84), channel_id=1, source_target_pairs={{4,0},{8,4},{12,8},{16,12},{20,16},{24,20},{28,24},{5,1},{9,5},{13... | collective-permute-start | bytes 165896 | tf_op jit(solution)/shard_map/ppermute | solution.py:18
  372.5 133.4 %all-reduce.24.cloned.1.call-start = ((), (), s32[]{:S(2)}) async-start(), calls=%async_computation.3 | async-start | bytes 589824 | tf_op jit(solution)/shard_map/psum | solution.py:198
Sparse Core Ops, SparseCore 0:
  46.4 91.4 all-gather.6
  210.5 88.9 all-gather.4
  372.7 77.3 all-reduce.21
  453.0 52.8 all-reduce.23
